TPU v7x, 512 devices: a whole 4x4x16 slice. The times are simulated.
512 devices in a mesh: pts: 64 (over x, z), cand: 8 (over y, core).
Axes of the slice: x: 4, y: 4, z: 16, core: 2. Of those that a mesh axis runs over, the one named last changes fastest.
Arguments:
- points: bfloat16 [32768, 4096], P('pts'), may hold values from -6 to 6
- weights: float32 [32768], P('pts'), may hold values from 0.25 to 4
- coverage: float32 [32768], P('pts'), may hold values from 0 to 1.5
- cand_index: int32 [2, 4096], P(None, 'pts'), may hold values from 0 to 511
- winners: int32 [2], replicated, may hold values from 0 to 4095
Outputs:
- gains: float32 [2, 4096], P(None, ('pts', 'cand'))
- final_cover: float32 [32768], P('pts')
All inputs are finite; a program needn't handle non-finite values.
Results may differ from a plain program's by a relative error of at most 0.0003.
Values may be sent and summed in bfloat16 or wider, within the bound.
No kernel may reach another device: no remote copies, remote signals or barrier semaphores. Data moves between devices by JAX's collectives and lax.ppermute only.
A program may use at most 64 MiB of HBM per device.

v0:
```python
import jax
import jax.numpy as jnp
from jax import lax
from jax.sharding import Mesh
from jax.sharding import PartitionSpec as P

PTS = ("pts_0", "pts_1")
PTS_CAND = ("pts_0", "pts_1", "cand")
LIFT = 2.0**13


def body(points, weights, coverage, cand_index, winners):
    rows_dev, width = points.shape
    steps, per_row = cand_index.shape
    n_x, n_z = (lax.axis_size(axis) for axis in PTS)
    n_cand = lax.axis_size("cand")
    per_dev = per_row // n_cand
    held = steps * per_dev
    total = float(rows_dev * n_x * n_z)
    scale = width ** (-0.5) / LIFT
    my_cand = lax.axis_index("cand")
    my_pts = lax.axis_index(PTS)
    mine = lax.dynamic_slice_in_dim(cand_index, my_cand * per_dev, per_dev, 1).reshape(-1)
    owner = winners // per_row
    won = jnp.take_along_axis(cand_index, (winners % per_row)[:, None], axis=1)[:, 0]
    won = jnp.where(owner == my_pts, won, -1)
    wanted = jnp.concatenate([mine, won])
    pick = jnp.where(
        wanted[:, None] == lax.broadcasted_iota(jnp.int32, (held + steps, rows_dev), 1), LIFT, 0.0
    ).astype(points.dtype)
    picked = lax.dot_general(
        pick, points, (((1,), (0,)), ((), ())), preferred_element_type=jnp.float32
    ).astype(jnp.float16)
    piece = steps * width // held
    sent = jnp.concatenate([picked[:held], picked[held:].reshape(held, piece)], axis=1)
    along_z = lax.all_gather(sent, PTS[1], axis=0, tiled=True)
    owner_x, owner_z = (owner // n_z, owner % n_z)
    part = held // steps
    chosen = [
        lax.dynamic_slice(along_z, (owner_z[t] * held + t * part, width), (part, piece)).reshape(
            1, width
        )
        for t in range(steps)
    ]
    pad = jnp.zeros((8 - steps, width), jnp.float16)
    column = jnp.concatenate([along_z[:, :width], *chosen, pad], axis=0)
    column_rows = n_z * held + 8
    block = lax.all_gather(column, PTS[0], axis=0, tiled=True).astype(points.dtype)
    block = block.reshape(n_x, column_rows, width)
    chosen = jnp.concatenate(
        [
            lax.dynamic_slice(block, (owner_x[t], n_z * held + t, 0), (1, 1, width))[0]
            for t in range(steps)
        ]
    )
    near = (
        lax.dot_general(
            points, chosen, (((1,), (1,)), ((), ())), preferred_element_type=jnp.float32
        )
        * scale
    )
    covers = [coverage]
    for t in range(steps):
        covers.append(jnp.maximum(covers[-1], near[:, t]))
    step_of = lax.broadcasted_iota(jnp.int32, (1, 1, n_z * held), 2) % held // per_dev
    cover = covers[0][:, None, None]
    for t in range(1, steps):
        cover = jnp.where(step_of >= t, covers[t][:, None, None], cover)
    sim = (
        lax.dot_general(
            points,
            block[:, : n_z * held],
            (((1,), (2,)), ((), ())),
            preferred_element_type=jnp.float32,
        )
        * scale
    )
    part = jnp.sum(weights[:, None, None] * jnp.maximum(sim - cover, 0.0), axis=0)
    part = lax.all_to_all(part.reshape(n_x * n_z, held), PTS, 0, 0, tiled=True)
    gains = jnp.sum(part, axis=0) / total
    return (gains.reshape(steps, per_dev), covers[-1])


def solution(mesh):
    torus = Mesh(mesh.devices.reshape(4, 16, mesh.shape["cand"]), ("pts_0", "pts_1", "cand"))
    in_specs = (P(PTS, None), P(PTS), P(PTS), P(None, PTS), P())
    out_specs = (P(None, PTS_CAND), P(PTS))
    return jax.shard_map(body, mesh=torus, in_specs=in_specs, out_specs=out_specs, check_vma=False)
```

profile of v0, /device:TPU:24, one launch (start us, length us, event | category | flops | bytes accessed | tf_op | source)
XLA Modules:
  0.0 183.7 jit_solution(2298904888433843876)
XLA Ops:
  0.6 0.0 copy-start
  0.7 0.7 and_select_fusion
  1.4 0.1 copy.9
  1.4 0.2 or_reduce_fusion
  1.6 0.0 copy-done
  1.6 0.6 gather_fusion
  2.3 0.1 constant_dynamic-slice_fusion
  2.4 0.1 reshape.151
  2.4 0.1 pad_add_fusion.1
  2.5 2.9 %convolution_convert_fusion = f16[18,4096]{1,0:T(8,128)(2,1)S(1)} fusion(bf16[512,4096]{1,0:T(8,128)(2,1)} %param.5, s32[18]{0:T(128)S(1)} %pad_add_fusion.1), kind=kOutput, calls=%fused_computation.3 | convolution fusion | flops 75598848 | bytes 4341832 | tf_op jit(solution)/shard_map/dot_general | solution.py:31
  5.5 0.6 fusion.23
  8.6 51.8 %all-gather.2 = f16[256,4608]{1,0:T(8,128)(2,1)S(1)} all-gather(f16[16,4608]{1,0:T(8,128)(2,1)S(1)} %pad_maximum_fusion), channel_id=1, replica_groups=mesh['pts_0'=4,'pts_1'=16,'cand'=8] {'pts_1'}, dimensions={0}, use_global_device_ids=true | all-gather | bytes 2506752 | tf_op jit(solution)/shard_map/all_gather | solution.py:36
  60.5 0.6 fusion.24
  62.3 1.7 slice.44
  64.1 0.1 pad.5.clone
  64.2 2.4 %maximum_maximum_fusion = f16[264,4096]{1,0:T(8,128)(2,1)S(1)} fusion(f16[1,4096]{1,0:T(2,128)(2,1)S(1)} %bitcast.44, f16[1,4096]{1,0:T(2,128)(2,1)S(1)} %bitcast.43, f16[256,4096]{1,0:T(8,128)(2,1)} %slice.44, f16[264]{0:T(512)(128)(2,1)S(1)} %pad.5.clone), kind=kLoop, calls=%fused_computation.5 | loop fusion | flops 3244032 | bytes 4276752 | tf_op jit(solution)/shard_map/concatenate | solution.py:46
  66.6 68.2 %all-gather.3 = f16[1056,4096]{1,0:T(8,128)(2,1)} all-gather(f16[264,4096]{1,0:T(8,128)(2,1)S(1)} %maximum_maximum_fusion), channel_id=1, replica_groups=mesh['pts_0'=4,'pts_1'=16,'cand'=8] {'pts_0'}, dimensions={0}, use_global_device_ids=true | all-gather | bytes 10813440 | tf_op jit(solution)/shard_map/all_gather | solution.py:48
  134.9 9.8 %convert_element_type.11 = bf16[1056,4096]{1,0:T(8,128)(2,1)} convert(f16[1056,4096]{1,0:T(8,128)(2,1)} %all-gather.3) | non-fusion elementwise | flops 4325376 | bytes 17301504 | tf_op jit(solution)/shard_map/convert_element_type | solution.py:48
  146.0 0.9 dynamic-slice_bitcast_fusion.1
  146.9 0.0 copy-start.1
  146.9 0.0 copy-start.3
  146.9 3.5 %fusion.10 = f32[512,2]{0,1:T(2,128)S(1)} fusion(bf16[512,4096]{1,0:T(8,128)(2,1)} %param.5, bf16[1,4096]{1,0:T(2,128)(2,1)S(1)} %get-tuple-element.7, bf16[1,4096]{1,0:T(2,128)(2,1)S(1)} %get-tuple-element.6), kind=kOutput, calls=%fused_computation.11 | convolution fusion | flops 8422400 | bytes 4214784 | tf_op jit(solution)/shard_map/dot_general | solution.py:57
  150.4 0.0 copy-done.2
  150.5 0.6 fusion.21
  151.0 0.1 broadcast_select_fusion
  151.1 0.0 copy-done.1
  151.2 0.0 copy-done.3
  151.2 8.1 %fusion.5 = f32[4,256]{1,0:T(4,128)S(1)} fusion(bf16[512,4096]{1,0:T(8,128)(2,1)S(1)} %copy-done.1, bf16[4,264,4096]{2,1,0:T(8,128)(2,1)} %bitcast.41, f32[512,256]{0,1:T(8,128)S(1)} %broadcast_select_fusion, f32[512]{0:T(512)S(1)} %copy-done.3), kind=kOutput, calls=%fused_computation.9 | convolution fusion | flops 4297587712 | bytes 13113344 | tf_op jit(solution)/shard_map/dot_general | solution.py:70
  159.3 0.1 all_to_all.6
  159.3 23.6 %all_to_all.9 = f32[64,1,16]{2,1,0:T(1,128)S(1)} all-to-all(f32[64,1,16]{2,1,0:T(1,128)S(1)} %bitcast.42), channel_id=1, replica_groups=mesh['pts_0'=4,'pts_1'=16,'cand'=8] {'pts_0','pts_1'}, dimensions={0} | all-to-all | bytes 8192 | tf_op jit(solution)/shard_map/all_to_all | solution.py:79
  183.0 0.1 reduce_sum.19
  183.1 0.6 div.52
  (15 shorter events, 0.2 us)
Async XLA Ops:
  0.6 1.0 copy-start
  144.7 5.7 %copy-start.2 = (f32[512]{0:T(512)S(1)}, f32[512]{0:T(512)}, u32[]{:S(2)}) copy-start(f32[512]{0:T(512)} %param.7) | copy-start | bytes 6148
  146.9 4.3 %copy-start.1 = (bf16[512,4096]{1,0:T(8,128)(2,1)S(1)}, bf16[512,4096]{1,0:T(8,128)(2,1)}, u32[]{:S(2)}) copy-start(bf16[512,4096]{1,0:T(8,128)(2,1)} %param.5) | copy-start | bytes 12582916
  146.9 4.3 %copy-start.3 = (f32[512]{0:T(512)S(1)}, f32[512]{0:T(512)}, u32[]{:S(2)}) copy-start(f32[512]{0:T(512)} %param.6) | copy-start | bytes 6148
where the time goes:
time: 184 us
  blocking collectives  144 us (78%)
  matrix products  14.5 us (8%)
  other arithmetic  14 us (8%)
  between operations  5.85 us (3%)
  local copies, waits for them, and re-layouts  5.64 us (3%)
    all_gather x1, blocking collectives, body(): lax.all_gather(column, PTS[0], axis=0, tiled=True).astype(points.dtype)  68.2 us
    all_gather x1, blocking collectives, body(): along_z = lax.all_gather(sent, PTS[1], axis=0, tiled=True)  51.8 us
    all_to_all x1, blocking collectives, body(): part = lax.all_to_all(part.reshape(n_x * n_z, held), PTS, 0, 0, tiled=True)  23.6 us
    convert_element_type x1, other arithmetic, body(): lax.all_gather(column, PTS[0], axis=0, tiled=True).astype(points.dtype)  9.84 us
    dot_general x1, matrix products, body(): lax.dot_general(points, block[:, :n_z * held], (((1,), (2,)), ((), ())),...  8.08 us

commit v1 on v0

--- a/solution.py
+++ b/solution.py
@@ -45,7 +45,16 @@
     pad = jnp.zeros((8 - steps, width), jnp.float16)
     column = jnp.concatenate([along_z[:, :width], *chosen, pad], axis=0)
     column_rows = n_z * held + 8
-    block = lax.all_gather(column, PTS[0], axis=0, tiled=True).astype(points.dtype)
+    note_the_cube = lambda here_x, shard_axis: jnp.concatenate(
+        lax.all_to_all(
+            jnp.stack([here_x for _ in range(lax.psum(1, axis_name=shard_axis))], axis=0),
+            axis_name=shard_axis,
+            split_axis=0,
+            concat_axis=0,
+        ),
+        0,
+    )
+    block = note_the_cube(column, PTS[0]).astype(points.dtype)
     block = block.reshape(n_x, column_rows, width)
     chosen = jnp.concatenate(
         [

time: 184 us -> 209 us (1.14)
  waiting for transfers between devices: 0 us -> 86.4 us
  blocking collectives: 144 us -> 74.2 us
  starting transfers between devices: 0 us -> 5.68 us
  local copies, waits for them, and re-layouts: 5.64 us -> 10.2 us
  matrix products: 14.5 us -> 12.2 us
    all_to_all x0 -> x1, waiting for transfers between devices: none -> 86.4 us  [body(): lax.all_to_all(jnp.stack([here_x for _ in range(lax.psum(1, axis_name=sha...]
    all_gather x1 -> x0, blocking collectives: 68.2 us -> none  [body(): lax.all_gather(column, PTS[0], axis=0, tiled=True).astype(points.dtype)]
    all_to_all x0 -> x1, starting transfers between devices: none -> 5.68 us  [body(): lax.all_to_all(jnp.stack([here_x for _ in range(lax.psum(1, axis_name=sha...]
    another operation x0 -> x1, local copies, waits for them, and re-layouts: none -> 4.52 us  [body(): jnp.stack([here_x for _ in range(lax.psum(1, axis_name=shard_axis))], axi...]
    dot_general x1, matrix products: 3.52 us -> 1.18 us  [body(): lax.dot_general(points, chosen, (((1,), (1,)), ((), ())), preferred_eleme...]
  transfers between devices with their start and end apart: 0 -> 1, of which waited for: 0 -> 1; matrix products, arithmetic and copies ran while one was open for 0% -> 0% of each run, Pallas kernels for 0% -> 0%
where the time goes in v1:
time: 209 us
  waiting for transfers between devices  86.4 us (41%)
  blocking collectives  74.2 us (36%)
  other arithmetic  14.2 us (7%)
  matrix products  12.2 us (6%)
  local copies, waits for them, and re-layouts  10.2 us (5%)
  between operations  5.97 us (3%)
  starting transfers between devices  5.68 us (3%)
    all_to_all x1, waiting for transfers between devices, body(): lax.all_to_all(jnp.stack([here_x for _ in range(lax.psum(1, axis_name=sha...  86.4 us
    all_gather x1, blocking collectives, body(): along_z = lax.all_gather(sent, PTS[1], axis=0, tiled=True)  51.8 us
    all_to_all x1, blocking collectives, body(): part = lax.all_to_all(part.reshape(n_x * n_z, held), PTS, 0, 0, tiled=True)  22.4 us
    convert_element_type x1, other arithmetic, body(): block = note_the_cube(column, PTS[0]).astype(points.dtype)  10 us
    dot_general x1, matrix products, body(): lax.dot_general(points, block[:, :n_z * held], (((1,), (2,)), ((), ())),...  8.16 us
    all_to_all x1, starting transfers between devices, body(): lax.all_to_all(jnp.stack([here_x for _ in range(lax.psum(1, axis_name=sha...  5.68 us
    another operation x1, local copies, waits for them, and re-layouts, body(): jnp.stack([here_x for _ in range(lax.psum(1, axis_name=shard_axis))], axi...  4.52 us
  transfers between devices with their start and end apart: 1, of which 1 were waited for; matrix products, arithmetic and copies ran while one was open for 0% of the time, Pallas kernels for 0%

profile of v1, /device:TPU:24, one launch (start us, length us, event | category | flops | bytes accessed | tf_op | source)
XLA Modules:
  0.0 208.9 jit_solution(4316902553373238681)
XLA Ops:
  0.6 0.0 copy-start
  0.7 0.7 and_select_fusion
  1.4 0.1 copy.9
  1.4 0.2 or_reduce_fusion
  1.6 0.0 copy-done
  1.6 0.6 gather_fusion
  2.3 0.1 constant_dynamic-slice_fusion
  2.4 0.1 reshape.152
  2.4 0.1 pad_add_fusion.1
  2.5 2.9 %convolution_convert_fusion = f16[18,4096]{1,0:T(8,128)(2,1)S(1)} fusion(bf16[512,4096]{1,0:T(8,128)(2,1)} %param.5, s32[18]{0:T(128)S(1)} %pad_add_fusion.1), kind=kOutput, calls=%fused_computation.3 | convolution fusion | flops 75598848 | bytes 4341832 | tf_op jit(solution)/shard_map/dot_general | solution.py:31
  5.5 51.8 %all-gather.1 = f16[256,4608]{1,0:T(8,128)(2,1)S(1)} all-gather(f16[16,4608]{1,0:T(8,128)(2,1)S(1)} %pad_maximum_fusion), channel_id=1, replica_groups=mesh['pts_0'=4,'pts_1'=16,'cand'=8] {'pts_1'}, dimensions={0}, use_global_device_ids=true | all-gather | bytes 2506752 | tf_op jit(solution)/shard_map/all_gather | solution.py:36
  57.4 0.6 fusion.24
  59.3 1.7 slice.44
  61.1 0.1 pad.5.clone
  61.1 2.4 %maximum_maximum_fusion = f16[264,4096]{1,0:T(8,128)(2,1)S(1)} fusion(f16[1,4096]{1,0:T(2,128)(2,1)S(1)} %bitcast.41, f16[1,4096]{1,0:T(2,128)(2,1)S(1)} %bitcast.40, f16[256,4096]{1,0:T(8,128)(2,1)} %slice.44, f16[264]{0:T(512)(128)(2,1)S(1)} %pad.5.clone), kind=kLoop, calls=%fused_computation.5 | loop fusion | flops 3244032 | bytes 4276752 | tf_op jit(solution)/shard_map/concatenate | solution.py:46
  63.6 4.5 %stack.2 = f16[4,264,4096]{2,1,0:T(8,128)(2,1)} broadcast(f16[264,4096]{1,0:T(8,128)(2,1)S(1)} %maximum_maximum_fusion), dimensions={1,2} | broadcast | bytes 10813440 | tf_op jit(solution)/shard_map/stack | solution.py:50
  68.1 5.7 %all-to-all-start = ((f16[4,264,4096]{2,1,0:T(8,128)(2,1)}), f16[4,264,4096]{2,1,0:T(8,128)(2,1)}, u32[]{:S(2)}, u32[]{:S(2)}) async-start(f16[4,264,4096]{2,1,0:T(8,128)(2,1)} %stack.2), calls=%async_computation | async-start | bytes 17301504 | tf_op jit(solution)/shard_map/all_to_all | solution.py:49
  73.8 0.6 fusion.23
  78.3 86.4 %all-to-all-done = f16[4,264,4096]{2,1,0:T(8,128)(2,1)} async-done(((f16[4,264,4096]{2,1,0:T(8,128)(2,1)}), f16[4,264,4096]{2,1,0:T(8,128)(2,1)}, u32[]{:S(2)}, u32[]{:S(2)}) %all-to-all-start) | async-done | bytes 8650784 | tf_op jit(solution)/shard_map/all_to_all | solution.py:49
  164.6 10.0 %convert_element_type.12 = bf16[4,264,4096]{2,1,0:T(8,128)(2,1)} convert(f16[4,264,4096]{2,1,0:T(8,128)(2,1)} %all-to-all-done) | non-fusion elementwise | flops 4325376 | bytes 17301504 | tf_op jit(solution)/shard_map/convert_element_type | solution.py:57
  174.7 0.9 dynamic-slice_bitcast_fusion.1
  175.6 0.0 copy-done.1
  175.6 0.0 copy-start.3
  175.6 1.2 fusion.10
  176.8 0.0 copy-done.2
  176.8 0.6 fusion.21
  177.4 0.1 broadcast_select_fusion
  177.5 8.2 %fusion.5 = f32[4,256]{1,0:T(4,128)S(1)} fusion(bf16[512,4096]{1,0:T(8,128)(2,1)S(1)} %copy-done.1, bf16[4,264,4096]{2,1,0:T(8,128)(2,1)} %convert_element_type.12, f32[512,256]{0,1:T(8,128)S(1)} %broadcast_select_fusion, f32[512]{0:T(512)S(1)} %copy-done.3), kind=kOutput, calls=%fused_computation.9 | convolution fusion | flops 4297587712 | bytes 13113344 | tf_op jit(solution)/shard_map/dot_general | solution.py:79
  185.7 0.1 all_to_all.10
  185.7 22.4 %all_to_all.14 = f32[64,1,16]{2,1,0:T(1,128)S(1)} all-to-all(f32[64,1,16]{2,1,0:T(1,128)S(1)} %bitcast.39), channel_id=1, replica_groups=mesh['pts_0'=4,'pts_1'=16,'cand'=8] {'pts_0','pts_1'}, dimensions={0} | all-to-all | bytes 8192 | tf_op jit(solution)/shard_map/all_to_all | solution.py:88
  208.2 0.1 reduce_sum.19
  208.2 0.6 div.52
  (17 shorter events, 0.2 us)
Async XLA Ops:
  0.6 1.0 copy-start
  68.1 96.6 %all-to-all-start = ((f16[4,264,4096]{2,1,0:T(8,128)(2,1)}), f16[4,264,4096]{2,1,0:T(8,128)(2,1)}, u32[]{:S(2)}, u32[]{:S(2)}) async-start(f16[4,264,4096]{2,1,0:T(8,128)(2,1)} %stack.2), calls=%async_computation | async-start | bytes 17301504 | tf_op jit(solution)/shard_map/all_to_all | solution.py:49
  164.6 10.9 %copy-start.1 = (bf16[512,4096]{1,0:T(8,128)(2,1)S(1)}, bf16[512,4096]{1,0:T(8,128)(2,1)}, u32[]{:S(2)}) copy-start(bf16[512,4096]{1,0:T(8,128)(2,1)} %param.5) | copy-start | bytes 12582916
  174.7 2.1 %copy-start.2 = (f32[512]{0:T(512)S(1)}, f32[512]{0:T(512)}, u32[]{:S(2)}) copy-start(f32[512]{0:T(512)} %param.7) | copy-start | bytes 6148
  175.6 1.9 copy-start.3
